TPU v7x, 512 devices: a whole 4x8x8 slice. The times are simulated.
512 devices in a mesh: seq: 64 (over z, y), head: 8 (over x, core).
Axes of the slice: x: 4, y: 8, z: 8, core: 2. Of those that a mesh axis runs over, the one named last changes fastest.
Arguments:
- queries: bfloat16 [9216, 8192], P('seq', 'head'), may hold values from -24 to 24
- key_matrix: bfloat16 [9216, 1024], P('seq', 'head'), may hold values from -4 to 4
- value_matrix: bfloat16 [9216, 1024], P('seq', 'head'), may hold values from -6 to 6
- query_feature_weight: bfloat16 [128, 4096], P(None, 'head'), may hold values from -0.5 to 0.5
- key_feature_weight: bfloat16 [128, 512], P(None, 'head'), may hold values from -0.5 to 0.5
Outputs:
- student_out: bfloat16 [9216, 8192], P('seq', 'head')
- query_map_grad: float32 [128, 4096], P(None, 'head')
- key_weight_gradient: float32 [128, 512], P(None, 'head')
- transfer_loss: float32 [], replicated
All inputs are finite; a program needn't handle non-finite values.
Results may differ from a plain program's by a relative error of at most 0.008.
Values may be sent and summed in bfloat16 or wider, within the bound.
A program may use at most 128 MiB of HBM per device.

v0:
```python
import jax
import jax.numpy as jnp
from jax import lax
from jax.sharding import PartitionSpec as P

HEAD_SIZE = 128
GROUP_QUERIES = 8
HALF_FEATURES = 64
NEG_LARGE = -1e30


def prefix(shard, axis, join, neutral, backward):
    count = lax.axis_size(axis)
    place = lax.axis_index(axis)
    ahead = count - 1 - place if backward else place
    gathered = jax.tree.map(
        lambda a, kind: lax.all_gather(a.astype(kind), axis), shard, (jnp.bfloat16, jnp.bfloat16)
    )
    state = jax.tree.map(lambda a, e: jnp.zeros_like(a) + jnp.asarray(e, a.dtype), shard, neutral)

    def one(lap, state):
        source = count - 1 - lap if backward else lap
        return join(
            state,
            jax.tree.map(
                lambda a, own: lax.dynamic_index_in_dim(a, source, 0, False).astype(own.dtype),
                gathered,
                shard,
            ),
        )

    return lax.fori_loop(0, ahead, one, state)


def feature_pair(logits):
    plus_half = jax.nn.softmax(logits, axis=-1)
    minus_half = jax.nn.softmax(-logits, axis=-1)
    return (plus_half, minus_half)


def pair_backward(plus_half, minus_half, d_features):
    feat_count = plus_half.shape[-1]
    d_plus = d_features[..., :feat_count]
    d_minus = d_features[..., feat_count:]
    inner_plus = jnp.sum(d_plus * plus_half, axis=-1, keepdims=True)
    inner_minus = jnp.sum(d_minus * minus_half, axis=-1, keepdims=True)
    return plus_half * (d_plus - inner_plus) - minus_half * (d_minus - inner_minus)


def add_pair(earlier_pair, later_pair):
    return (earlier_pair[0] + later_pair[0], earlier_pair[1] + later_pair[1])


def attend(running, row_block, query_pos, key_view, value_view, key_pos, score_scale):
    row_max, row_sum, weighted = running
    scores = (
        jnp.einsum("rkgd,lkd->kgrl", row_block, key_view, preferred_element_type=jnp.float32)
        * score_scale
    )
    visible = key_pos[None, None, None, :] <= query_pos[None, None, :, None]
    masked = jnp.where(visible, scores, NEG_LARGE)
    new_max = jnp.maximum(row_max, jnp.max(masked, axis=-1))
    exponent = jnp.where(visible, jnp.exp(masked - new_max[..., None]), 0.0)
    weights = exponent.astype(jnp.bfloat16)
    weighted = jnp.einsum("kgrl,lkd->kgrd", weights, value_view, preferred_element_type=jnp.float32)
    row_sum = jnp.sum(exponent, axis=-1)
    return (new_max, row_sum, weighted)


def local(queries, key_matrix, value_matrix, query_feature_weight, key_feature_weight):
    token_rows = queries.shape[0]
    local_heads = key_matrix.shape[1] // HEAD_SIZE
    seq_count = lax.axis_size("seq")
    position = lax.axis_index("seq")
    first_row = position * token_rows
    seg_total = token_rows * seq_count
    score_scale = HEAD_SIZE ** (-0.5)
    query_heads = queries.reshape(token_rows, local_heads, GROUP_QUERIES, HEAD_SIZE)
    key_heads = key_matrix.reshape(token_rows, local_heads, HEAD_SIZE)
    value_heads = value_matrix.reshape(token_rows, local_heads, HEAD_SIZE)
    query_map_view = query_feature_weight.reshape(
        HEAD_SIZE, local_heads, GROUP_QUERIES, HALF_FEATURES
    )
    key_map_view = key_feature_weight.reshape(HEAD_SIZE, local_heads, HALF_FEATURES)
    query_sets = ((query_heads, first_row + jnp.arange(token_rows, dtype=jnp.int32)),)

    def fresh_carry(row_block):
        row_count = row_block.shape[0]
        return (
            jnp.full((local_heads, GROUP_QUERIES, row_count), NEG_LARGE, jnp.float32),
            jnp.zeros((local_heads, GROUP_QUERIES, row_count), jnp.float32),
            jnp.zeros((local_heads, GROUP_QUERIES, row_count, HEAD_SIZE), jnp.float32),
        )

    first_key = jnp.int32(0)
    key_block = lax.all_gather(key_matrix, "seq", axis=0, tiled=True)
    value_block = lax.all_gather(value_matrix, "seq", axis=0, tiled=True)
    key_count = key_block.shape[0]
    key_view = key_block.reshape(key_count, local_heads, HEAD_SIZE)
    value_view = value_block.reshape(key_count, local_heads, HEAD_SIZE)
    key_pos = jnp.arange(key_count, dtype=jnp.int32)
    teach_runs = tuple((fresh_carry(query_set[0]) for query_set in query_sets))
    updated = []
    for query_set, fold_teach_run in zip(query_sets, teach_runs):
        row_block, query_pos = query_set

        def visit_block(current, row_block=row_block, query_pos=query_pos):
            return attend(current, row_block, query_pos, key_view, value_view, key_pos, score_scale)

        def unchanged(current):
            return current

        updated.append(lax.cond(first_key <= query_pos[-1], visit_block, unchanged, fold_teach_run))
    teach_done = tuple(updated)

    def finish(teach_run):
        return (teach_run[2] / teach_run[1][..., None]).astype(jnp.bfloat16)

    finished = [finish(teach_run) for teach_run in teach_done]
    teacher = finished[0]
    query_logits = jnp.einsum(
        "tkgd,dkgf->kgtf", query_heads, query_map_view, preferred_element_type=jnp.float32
    )
    query_plus, query_minus = feature_pair(query_logits)
    query_phi = jnp.concatenate([query_plus, query_minus], axis=-1).astype(jnp.bfloat16)
    logits = jnp.einsum("lkd,dkf->klf", key_heads, key_map_view, preferred_element_type=jnp.float32)
    plus_half, minus_half = feature_pair(logits)
    key_phi = jnp.concatenate([plus_half, minus_half], axis=-1).astype(jnp.bfloat16)
    block_state = jnp.einsum(
        "ktf,tkd->kfd", key_phi, value_heads, preferred_element_type=jnp.float32
    )
    block_norm = jnp.sum(key_phi.astype(jnp.float32), axis=1)
    zero_pair = (jnp.zeros_like(block_state), jnp.zeros_like(block_norm))
    prefix_state, prefix_norm = prefix((block_state, block_norm), "seq", add_pair, zero_pair, False)
    prefix_low = prefix_state.astype(jnp.bfloat16)
    token_index = jnp.arange(token_rows, dtype=jnp.int32)
    causal = token_index[None, :] <= token_index[:, None]
    intra_scores = jnp.where(
        causal,
        jnp.einsum("kgtf,ksf->kgts", query_phi, key_phi, preferred_element_type=jnp.float32),
        0.0,
    )
    numerator = jnp.einsum(
        "kgts,skd->kgtd",
        intra_scores.astype(jnp.bfloat16),
        value_heads,
        preferred_element_type=jnp.float32,
    )
    numerator = numerator + jnp.einsum(
        "kgtf,kfd->kgtd", query_phi, prefix_low, preferred_element_type=jnp.float32
    )
    query_wide = query_phi.astype(jnp.float32)
    denominator = jnp.sum(intra_scores, axis=-1) + jnp.einsum(
        "kgtf,kf->kgt", query_wide, prefix_norm, precision=lax.Precision.HIGHEST
    )
    student = numerator / denominator[..., None]
    target = teacher.astype(jnp.float32)
    differ = student - target
    loss_local = jnp.sum(differ * differ)
    grad_out = 2.0 * differ / seg_total
    numer_grad = grad_out / denominator[..., None]
    denom_grad = -jnp.sum(grad_out * student, axis=-1) / denominator
    numer_low = numer_grad.astype(jnp.bfloat16)
    coupling = (
        jnp.einsum("kgtd,skd->kgts", numer_low, value_heads, preferred_element_type=jnp.float32)
        + denom_grad[..., None]
    )
    coupling_low = jnp.where(causal, coupling, 0.0).astype(jnp.bfloat16)
    later_state = jnp.einsum(
        "kgtf,kgtd->kfd", query_phi, numer_low, preferred_element_type=jnp.float32
    )
    later_norm = jnp.einsum("kgtf,kgt->kf", query_wide, denom_grad, precision=lax.Precision.HIGHEST)
    zero_later = (jnp.zeros_like(later_state), jnp.zeros_like(later_norm))
    suffix_state, suffix_norm = prefix((later_state, later_norm), "seq", add_pair, zero_later, True)
    suffix_low = suffix_state.astype(jnp.bfloat16)
    query_dphi = jnp.einsum(
        "kgts,ksf->kgtf", coupling_low, key_phi, preferred_element_type=jnp.float32
    )
    query_dphi = query_dphi + jnp.einsum(
        "kgtd,kfd->kgtf", numer_low, prefix_low, preferred_element_type=jnp.float32
    )
    query_dphi = query_dphi + denom_grad[..., None] * prefix_norm[:, None, None, :]
    key_dphi = jnp.einsum(
        "kgts,kgtf->ksf", coupling_low, query_phi, preferred_element_type=jnp.float32
    )
    key_dphi = key_dphi + jnp.einsum(
        "skd,kfd->ksf", value_heads, suffix_low, preferred_element_type=jnp.float32
    )
    key_dphi = key_dphi + suffix_norm[:, None, :]
    query_dlogit = pair_backward(query_plus, query_minus, query_dphi).astype(jnp.bfloat16)
    key_dlogit = pair_backward(plus_half, minus_half, key_dphi).astype(jnp.bfloat16)
    query_grad = jnp.einsum(
        "tkgd,kgtf->dkgf", query_heads, query_dlogit, preferred_element_type=jnp.float32
    )
    key_grad = jnp.einsum("tkd,ktf->dkf", key_heads, key_dlogit, preferred_element_type=jnp.float32)
    query_grad, key_grad = lax.psum((query_grad, key_grad), "seq")
    transfer_loss = lax.psum(loss_local, ("seq", "head")) / seg_total
    student_out = (
        student.astype(jnp.bfloat16)
        .transpose(2, 0, 1, 3)
        .reshape(token_rows, local_heads * GROUP_QUERIES * HEAD_SIZE)
    )
    return (
        student_out,
        query_grad.reshape(HEAD_SIZE, local_heads * GROUP_QUERIES * HALF_FEATURES),
        key_grad.reshape(HEAD_SIZE, local_heads * HALF_FEATURES),
        transfer_loss,
    )


def solution(mesh):
    placed = (
        P("seq", "head"),
        P("seq", "head"),
        P("seq", "head"),
        P(None, "head"),
        P(None, "head"),
    )
    return jax.shard_map(
        local,
        mesh=mesh,
        in_specs=placed,
        out_specs=(P("seq", "head"), P(None, "head"), P(None, "head"), P()),
        check_vma=False,
    )
```

profile of v0, /device:TPU:2, one launch (start us, length us, event | category | flops | bytes accessed | tf_op | source)
XLA Modules:
  0.0 812.8 jit_solution(13775298181172924217)
XLA Ops:
  7.9 0.9 fusion.99
  8.9 1.5 convolution_convert_fusion
  13.4 1.0 copy.51
  14.5 49.8 %all-gather.4 = bf16[64,1,128]{2,1,0:T(2,128)(2,1)S(1)} all-gather(bf16[1,1,128]{2,1,0:T(2,128)(2,1)S(1)} %bitcast.271), channel_id=3, replica_groups=mesh['seq'=64,'head'=8] {'seq'}, dimensions={0}, use_global_device_ids=true | all-gather | bytes 16640 | tf_op jit(solution)/shard_map/all_gather | solution.py:17
  64.3 1.3 fusion.103
  65.7 1.3 fusion.100
  67.5 1.1 fusion.38
  68.7 31.2 %all-gather.15.cloned.1.call-done = bf16[8192,128]{1,0:T(8,128)(2,1)} async-done(((bf16[128,128]{1,0:T(8,128)(2,1)}), bf16[8192,128]{1,0:T(8,128)(2,1)}) %all-gather.15.cloned.1.call-update) | async-done | bytes 2097168 | tf_op jit(solution)/shard_map/all_gather | solution.py:17
  100.2 83.5 %all-gather.11.cloned.1.call-done = bf16[9216,128]{1,0:T(8,128)(2,1)} async-done(((bf16[144,128]{1,0:T(8,128)(2,1)}), bf16[9216,128]{1,0:T(8,128)(2,1)}) %all-gather.11.cloned.1.call-update) | async-done | bytes 2359312 | tf_op jit(solution)/shard_map/all_gather | solution.py:96
  183.7 83.7 %all-gather.13.cloned.1.call-done = bf16[9216,128]{1,0:T(8,128)(2,1)} async-done(((bf16[144,128]{1,0:T(8,128)(2,1)}), bf16[9216,128]{1,0:T(8,128)(2,1)}) %all-gather.13.cloned.1.call-update) | async-done | bytes 2359312 | tf_op jit(solution)/shard_map/all_gather | solution.py:97
  267.4 62.5 %conditional.1 = (f32[1,8,144]{2,1,0:T(8,128)}, f32[1,8,144,128]{3,2,1,0:T(8,128)}) conditional(s32[]{:T(128)} %bitcast.28, () %tuple.33, (s32[9216]{0:T(1024)S(1)}, s32[144]{0:T(256)}, bf16[144,1024]{1,0:T(8,128)(2,1)}, bf16[9216,128]{1,0:T(8,128)(2,1)}, bf16[9216,128]{1,0:T(8,128)(2,1)}) %tuple.98), branch_computations={%region_12.13_spmd, %region_13.16_spmd} | conditional | flops 5575162880 | bytes 138378832 | solution.py:113
  267.6 1.4 broadcast_compare_fusion
  269.0 18.7 %fusion = (f32[8,144]{1,0:T(8,128)S(1)}, f32[9216,144,8]{0,1,2:T(8,128)}) fusion(pred[144,9216]{1,0:T(8,128)(4,1)S(1)} %broadcast_compare_fusion, bf16[9216,128]{1,0:T(8,128)(2,1)} %get-tuple-element.118, bf16[144,1024]{1,0:T(8,128)(2,1)} %get-tuple-element.119), kind=kOutput, calls=%fused_computation.4 | convolution fusion | flops 2749758464 | bytes 46453248 | tf_op jit(solution)/shard_map/cond/branch_1_fun/rkgd,lkd->kgrl/dot_general | solution.py:57
  287.7 21.9 %fusion.2 = f32[8,144]{1,0:T(8,128)} fusion(f32[9216,144,8]{0,1,2:T(8,128)} %get-tuple-element.217, f32[8,144]{1,0:T(8,128)S(1)} %broadcast_maximum_fusion, pred[144,9216]{1,0:T(8,128)(4,1)S(1)} %broadcast_compare_fusion), kind=kLoop, calls=%fused_computation.6 | loop fusion | flops 53083008 | bytes 43803648 | tf_op jit(solution)/shard_map/cond/branch_1_fun/reduce_sum | solution.py:66
  309.6 20.2 %fusion.10 = f32[1,8,144,128]{3,2,1,0:T(8,128)} fusion(bf16[9216,128]{1,0:T(8,128)(2,1)} %get-tuple-element.120, f32[9216,144,8]{0,1,2:T(8,128)} %get-tuple-element.217, f32[8,144]{1,0:T(8,128)S(1)} %broadcast_maximum_fusion, pred[144,9216]{1,0:T(8,128)(4,1)S(1)} %broadcast_compare_fusion), kind=kOutput, calls=%fused_computation.14 | convolution fusion | flops 2770993152 | bytes 46748160 | tf_op jit(solution)/shard_map/cond/branch_1_fun/kgrl,lkd->kgrd/dot_general | solution.py:65
  329.9 2.8 multiply_reduce_fusion
  332.9 1.9 fusion.34
  334.9 95.5 %psum.23 = f32[]{:T(128)} all-reduce(f32[]{:T(128)} %get-tuple-element.183), channel_id=1, replica_groups=mesh['seq'=64,'head'=8] {'seq','head'}, use_global_device_ids=true, to_apply=%region_26.27 | all-reduce | flops 1 | bytes 8 | tf_op jit(solution)/shard_map/psum | solution.py:197
  432.8 0.8 copy.65
  434.1 42.6 %all-gather.5 = bf16[64,1,128]{2,1,0:T(2,128)(2,1)S(1)} all-gather(bf16[1,1,128]{2,1,0:T(2,128)(2,1)S(1)} %fusion.36), channel_id=5, replica_groups=mesh['seq'=64,'head'=8] {'seq'}, dimensions={0}, use_global_device_ids=true | all-gather | bytes 16640 | tf_op jit(solution)/shard_map/all_gather | solution.py:17
  477.8 51.3 %while.27 = (s32[]{:T(128)}, f32[1,128,128]{2,1,0:T(8,128)S(1)}, f32[1,128]{1,0:T(1,128)S(1)}, s32[]{:T(128)}, bf16[64,1,128,128]{3,2,1,0:T(8,128)(2,1)}, /*inde...) while((s32[]{:T(128)}, f32[1,128,128]{2,1,0:T(8,128)S(1)}, ...), condition=%wide.region_21.22_spmd, body=%wide.region_20.21_spmd.sunk | while | flops 33030 | bytes 165283 | solution.py:32
  477.8 0.8 convert_add_fusion.10
  478.6 0.8 convert_add_fusion.10
  479.4 0.8 convert_add_fusion.10
  480.2 0.8 convert_add_fusion.10
  481.1 0.8 convert_add_fusion.10
  481.9 0.8 convert_add_fusion.10
  482.7 0.8 convert_add_fusion.10
  483.5 0.8 convert_add_fusion.10
  484.3 0.8 convert_add_fusion.10
  485.1 0.8 convert_add_fusion.10
  485.9 0.8 convert_add_fusion.10
  486.8 0.8 convert_add_fusion.10
  487.6 0.8 convert_add_fusion.10
  488.4 0.8 convert_add_fusion.10
  489.2 0.8 convert_add_fusion.10
  490.0 0.8 convert_add_fusion.10
  490.8 0.8 convert_add_fusion.10
  491.6 0.8 convert_add_fusion.10
  492.5 0.8 convert_add_fusion.10
  493.3 0.8 convert_add_fusion.10
  494.1 0.8 convert_add_fusion.10
  494.9 0.8 convert_add_fusion.10
  495.7 0.8 convert_add_fusion.10
  497.3 0.8 convert_add_fusion.10
  498.2 0.8 convert_add_fusion.10
  499.0 0.8 convert_add_fusion.10
  501.4 0.8 convert_add_fusion.10
  502.2 0.8 convert_add_fusion.10
  503.9 0.8 convert_add_fusion.10
  504.7 0.8 convert_add_fusion.10
  505.5 0.8 convert_add_fusion.10
  507.9 0.8 convert_add_fusion.10
  508.8 0.8 convert_add_fusion.10
  509.6 0.8 convert_add_fusion.10
  511.2 0.8 convert_add_fusion.10
  512.0 0.8 convert_add_fusion.10
  519.3 0.8 convert_add_fusion.10
  521.0 0.8 convert_add_fusion.10
  522.6 0.8 convert_add_fusion.10
  524.2 0.8 convert_add_fusion.10
  525.9 0.8 convert_add_fusion.10
  529.5 274.0 %psum.22 = f32[128,64]{0,1:T(8,128)} all-reduce(f32[128,64]{0,1:T(8,128)S(1)} %convolution_bitcast_fusion.3), channel_id=1, replica_groups=mesh['seq'=64,'head'=8] {'seq'}, use_global_device_ids=true, to_apply=%region_24.25 | all-reduce | flops 8192 | bytes 65536 | tf_op jit(solution)/shard_map/psum | solution.py:196
  803.5 1.7 copy.144
  (155 shorter events, 25.8 us)
Async XLA Ops:
  7.2 0.7 copy-start
  7.2 92.6 %all-gather.15.cloned.1.call-start = ((), (), s32[]{:S(2)}) async-start(), calls=%async_computation.3 | async-start | bytes 2129920 | tf_op jit(solution)/shard_map/all_gather | solution.py:17
  8.8 4.5 copy-start.5
  8.9 4.4 copy-start.7
  8.9 4.4 copy-start.9
  10.5 173.1 %all-gather.11.cloned.1.call-start = ((), (), s32[]{:S(2)}) async-start(), calls=%async_computation | async-start | bytes 2396160 | tf_op jit(solution)/shard_map/all_gather | solution.py:96
  11.3 256.1 %all-gather.13.cloned.1.call-start = ((), (), s32[]{:S(2)}) async-start(), calls=%async_computation.1 | async-start | bytes 2396160 | tf_op jit(solution)/shard_map/all_gather | solution.py:97
  12.0 465.7 %all-gather.17.cloned.1.call-start = ((), (), s32[]{:S(2)}) async-start(), calls=%async_computation.4 | async-start | bytes 2129920 | tf_op jit(solution)/shard_map/all_gather | solution.py:17
  12.1 1.3 copy-start.11
  67.1 200.2 %copy-start.2 = (bf16[8,144,64]{1,2,0:T(8,128)(2,1)}, bf16[8,144,64]{1,2,0:T(8,128)(2,1)S(1)}, u32[]{:S(2)}) copy-start(bf16[8,144,64]{1,2,0:T(8,128)(2,1)S(1)} %get-tuple-element.233) | copy-start | bytes 442372
  267.4 163.9 %copy-start.1 = (bf16[144,128]{1,0:T(8,128)(2,1)S(1)}, bf16[144,128]{1,0:T(8,128)(2,1)}, u32[]{:S(2)}) copy-start(bf16[144,128]{1,0:T(8,128)(2,1)} %param.13) | copy-start | bytes 110596
  329.9 102.6 %copy-start.12 = (bf16[144,1024]{1,0:T(8,128)(2,1)S(1)}, bf16[144,1024]{1,0:T(8,128)(2,1)}, u32[]{:S(2)}) copy-start(bf16[144,1024]{1,0:T(8,128)(2,1)} %param.11) | copy-start | bytes 884740
  329.9 103.8 %copy-start.3 = (bf16[8,144,64]{1,2,0:T(8,128)(2,1)S(1)}, bf16[8,144,64]{1,2,0:T(8,128)(2,1)}, u32[]{:S(2)}) copy-start(bf16[8,144,64]{1,2,0:T(8,128)(2,1)} %copy-done.2) | copy-start | bytes 442372
  332.7 196.6 %copy-start.6 = (f32[144]{0:T(256)S(1)}, f32[144]{0:T(256)}, u32[]{:S(2)}) copy-start(f32[144]{0:T(256)} %copy-done.5) | copy-start | bytes 1732
  332.7 196.6 %copy-start.8 = (f32[144]{0:T(256)S(1)}, f32[144]{0:T(256)}, u32[]{:S(2)}) copy-start(f32[144]{0:T(256)} %copy-done.7) | copy-start | bytes 1732
  332.7 196.6 %copy-start.10 = (f32[144]{0:T(256)S(1)}, f32[144]{0:T(256)}, u32[]{:S(2)}) copy-start(f32[144]{0:T(256)} %copy-done.9) | copy-start | bytes 1732
  332.9 196.5 %copy-start.4 = (bf16[144,128]{1,0:T(8,128)(2,1)S(1)}, bf16[144,128]{1,0:T(8,128)(2,1)}, u32[]{:S(2)}) copy-start(bf16[144,128]{1,0:T(8,128)(2,1)} %param.12) | copy-start | bytes 110596
  334.8 468.7 %all-reduce.2.cloned.1.call-start = ((), (), s32[]{:S(2)}) async-start(), calls=%async_computation.2 | async-start | bytes 524288 | tf_op jit(solution)/shard_map/psum | solution.py:196
Sparse Core Ops, SparseCore 0:
  11.6 88.1 all-gather.14
  102.9 80.7 all-gather.10
  186.7 80.5 all-gather.12
  334.9 80.1 all-gather.16
  477.2 147.5 all-reduce.1
where the time goes:
time: 818 us; the launch traced here: 813 us
  blocking collectives  462 us (56%)
  waiting for transfers between devices  200 us (24%)
  other arithmetic  73.9 us (9%)
  matrix products  53 us (6%)
  between operations  16.5 us (2%)
    psum x1, blocking collectives, local(): query_grad, key_grad = lax.psum((query_grad, key_grad), 'seq')  274 us
    psum x1, blocking collectives, local(): transfer_loss = lax.psum(loss_local, ('seq', 'head')) / seg_total  95.5 us
    all_gather x2, blocking collectives, prefix(): lax.all_gather(a.astype(kind), axis)  92.4 us
    all_gather x1, waiting for transfers between devices, local(): value_block = lax.all_gather(value_matrix, 'seq', axis=0, tiled=True)  83.7 us
    all_gather x1, waiting for transfers between devices, local(): key_block = lax.all_gather(key_matrix, 'seq', axis=0, tiled=True)  83.5 us
    add x126, other arithmetic, add_pair(): return (earlier_pair[0] + later_pair[0], earlier_pair[1] + later_pair[1])  49.7 us
    all_gather x2, waiting for transfers between devices, prefix(): lax.all_gather(a.astype(kind), axis)  31.2 us
    reduce_sum x1, other arithmetic, attend(): row_sum = jnp.sum(exponent, axis=-1)  21.9 us
  transfers between devices with their start and end apart: 5, of which 3 were waited for; matrix products, arithmetic and copies ran while one was open for 7% of the time, Pallas kernels for 0%

commit v1 on v0

--- a/solution.py
+++ b/solution.py
@@ -94,7 +94,10 @@
 
     first_key = jnp.int32(0)
     key_block = lax.all_gather(key_matrix, "seq", axis=0, tiled=True)
-    value_block = lax.all_gather(value_matrix, "seq", axis=0, tiled=True)
+    r1 = jax.lax.axis_size("seq")
+    passed = jnp.stack([value_matrix] * r1)
+    part_now = jax.lax.all_to_all(passed, axis_name="seq", split_axis=0, concat_axis=0)
+    value_block = jnp.concatenate(part_now, 0)
     key_count = key_block.shape[0]
     key_view = key_block.reshape(key_count, local_heads, HEAD_SIZE)
     value_view = value_block.reshape(key_count, local_heads, HEAD_SIZE)

time: 818 us -> 782 us (0.956)
  waiting for transfers between devices: 200 us -> 104 us
  blocking collectives: 462 us -> 503 us
  starting transfers between devices: 0.2 us -> 17 us
    all_gather x1 -> x0, waiting for transfers between devices: 83.7 us -> none  [local(): value_block = lax.all_gather(value_matrix, 'seq', axis=0, tiled=True)]
    all_gather x2, blocking collectives: 92.4 us -> 134 us  [prefix(): lax.all_gather(a.astype(kind), axis)]
    all_to_all x0 -> x1, starting transfers between devices: none -> 16.8 us  [local(): jax.lax.all_to_all(passed, axis_name='seq', split_axis=0, concat_axis=0)]
    all_gather x2, waiting for transfers between devices: 31.2 us -> 19.6 us  [prefix(): lax.all_gather(a.astype(kind), axis)]
  transfers between devices with their start and end apart: 5 -> 5, of which waited for: 3 -> 2; matrix products, arithmetic and copies ran while one was open for 7% -> 8% of each run, Pallas kernels for 0% -> 0%
where the time goes in v1:
time: 782 us; the launch traced here: 777 us
  blocking collectives  503 us (64%)
  waiting for transfers between devices  104 us (13%)
  other arithmetic  74.2 us (9%)
  matrix products  52.2 us (7%)
  starting transfers between devices  17 us (2%)
  between operations  16.5 us (2%)
  local copies, waits for them, and re-layouts  8.18 us (1%)
    psum x1, blocking collectives, local(): query_grad, key_grad = lax.psum((query_grad, key_grad), 'seq')  274 us
    all_gather x2, blocking collectives, prefix(): lax.all_gather(a.astype(kind), axis)  134 us
    psum x1, blocking collectives, local(): transfer_loss = lax.psum(loss_local, ('seq', 'head')) / seg_total  95.5 us
    all_gather x1, waiting for transfers between devices, local(): key_block = lax.all_gather(key_matrix, 'seq', axis=0, tiled=True)  83.6 us
    add x126, other arithmetic, add_pair(): return (earlier_pair[0] + later_pair[0], earlier_pair[1] + later_pair[1])  50 us
    reduce_sum x1, other arithmetic, attend(): row_sum = jnp.sum(exponent, axis=-1)  21.9 us
    dot_general x1, matrix products, attend(): jnp.einsum('kgrl,lkd->kgrd', weights, value_view, preferred_element_type=...  20.2 us
    all_gather x2, waiting for transfers between devices, prefix(): lax.all_gather(a.astype(kind), axis)  19.6 us
  transfers between devices with their start and end apart: 5, of which 2 were waited for; matrix products, arithmetic and copies ran while one was open for 8% of the time, Pallas kernels for 0%

profile of v1, /device:TPU:2, one launch (start us, length us, event | category | flops | bytes accessed | tf_op | source)
XLA Modules:
  0.0 777.1 jit_solution(14545461984367511052)
XLA Ops:
  7.9 0.9 fusion.96
  8.9 1.5 convolution_convert_fusion
  11.3 2.5 stack.2
  13.8 16.8 %all-to-all-start = ((bf16[64,144,128]{2,1,0:T(8,128)(2,1)}), bf16[64,144,128]{2,1,0:T(8,128)(2,1)}, u32[]{:S(2)}, u32[]{:S(2)}) async-start(bf16[64,144,128]{2,1,0:T(8,128)(2,1)} %stack.2), calls=%async_computation | async-start | bytes 4718592 | tf_op jit(solution)/shard_map/all_to_all | solution.py:99
  31.9 1.0 copy.51
  33.1 91.3 %all-gather.4 = bf16[64,1,128]{2,1,0:T(2,128)(2,1)S(1)} all-gather(bf16[1,1,128]{2,1,0:T(2,128)(2,1)S(1)} %bitcast.270), channel_id=3, replica_groups=mesh['seq'=64,'head'=8] {'seq'}, dimensions={0}, use_global_device_ids=true | all-gather | bytes 16640 | tf_op jit(solution)/shard_map/all_gather | solution.py:17
  124.4 1.3 fusion.100
  125.7 1.3 fusion.97
  128.0 19.6 %all-gather.12.cloned.1.call-done = bf16[8192,128]{1,0:T(8,128)(2,1)} async-done(((bf16[128,128]{1,0:T(8,128)(2,1)}), bf16[8192,128]{1,0:T(8,128)(2,1)}) %all-gather.12.cloned.1.call-update) | async-done | bytes 2097168 | tf_op jit(solution)/shard_map/all_gather | solution.py:17
  147.9 83.6 %all-gather.10.cloned.1.call-done = bf16[9216,128]{1,0:T(8,128)(2,1)} async-done(((bf16[144,128]{1,0:T(8,128)(2,1)}), bf16[9216,128]{1,0:T(8,128)(2,1)}) %all-gather.10.cloned.1.call-update) | async-done | bytes 2359312 | tf_op jit(solution)/shard_map/all_gather | solution.py:96
  231.5 62.5 %conditional.1 = (f32[1,8,144]{2,1,0:T(8,128)}, f32[1,8,144,128]{3,2,1,0:T(8,128)}) conditional(s32[]{:T(128)} %bitcast.29, () %tuple.33, (s32[9216]{0:T(1024)S(1)}, s32[144]{0:T(256)}, bf16[144,1024]{1,0:T(8,128)(2,1)}, bf16[9216,128]{1,0:T(8,128)(2,1)}, bf16[64,144,128]{2,1,0:T(8,128)(2,1)}) %tuple.96), branch_computations={%region_12.13_spmd, %region_13.16_spmd} | conditional | flops 5575162880 | bytes 138378832 | solution.py:116
  231.7 1.4 broadcast_compare_fusion
  233.2 18.7 %fusion = (f32[8,144]{1,0:T(8,128)S(1)}, f32[9216,144,8]{0,1,2:T(8,128)}) fusion(pred[144,9216]{1,0:T(8,128)(4,1)S(1)} %broadcast_compare_fusion, bf16[9216,128]{1,0:T(8,128)(2,1)} %get-tuple-element.118, bf16[144,1024]{1,0:T(8,128)(2,1)} %get-tuple-element.119), kind=kOutput, calls=%fused_computation.4 | convolution fusion | flops 2749758464 | bytes 46453248 | tf_op jit(solution)/shard_map/cond/branch_1_fun/rkgd,lkd->kgrl/dot_general | solution.py:57
  251.9 21.9 %fusion.2 = f32[8,144]{1,0:T(8,128)} fusion(f32[9216,144,8]{0,1,2:T(8,128)} %get-tuple-element.217, f32[8,144]{1,0:T(8,128)S(1)} %broadcast_maximum_fusion, pred[144,9216]{1,0:T(8,128)(4,1)S(1)} %broadcast_compare_fusion), kind=kLoop, calls=%fused_computation.6 | loop fusion | flops 53083008 | bytes 43803648 | tf_op jit(solution)/shard_map/cond/branch_1_fun/reduce_sum | solution.py:66
  273.8 20.2 %fusion.9 = f32[1,8,144,128]{3,2,1,0:T(8,128)} fusion(bf16[9216,128,1]{1,0,2:T(8,128)(2,1)} %bitcast.8, f32[9216,144,8]{0,1,2:T(8,128)} %get-tuple-element.217, f32[8,144]{1,0:T(8,128)S(1)} %broadcast_maximum_fusion, pred[144,9216]{1,0:T(8,128)(4,1)S(1)} %broadcast_compare_fusion), kind=kOutput, calls=%fused_computation.13 | convolution fusion | flops 2770993152 | bytes 46748160 | tf_op jit(solution)/shard_map/cond/branch_1_fun/kgrl,lkd->kgrd/dot_general | solution.py:65
  294.0 2.8 multiply_reduce_fusion
  297.1 1.9 fusion.31
  299.0 95.5 %psum.23 = f32[]{:T(128)} all-reduce(f32[]{:T(128)} %get-tuple-element.183), channel_id=1, replica_groups=mesh['seq'=64,'head'=8] {'seq','head'}, use_global_device_ids=true, to_apply=%region_26.27 | all-reduce | flops 1 | bytes 8 | tf_op jit(solution)/shard_map/psum | solution.py:200
  396.9 0.8 copy.65
  398.2 42.5 %all-gather.5 = bf16[64,1,128]{2,1,0:T(2,128)(2,1)S(1)} all-gather(bf16[1,1,128]{2,1,0:T(2,128)(2,1)S(1)} %fusion.33), channel_id=5, replica_groups=mesh['seq'=64,'head'=8] {'seq'}, dimensions={0}, use_global_device_ids=true | all-gather | bytes 16640 | tf_op jit(solution)/shard_map/all_gather | solution.py:17
  441.9 51.5 %while.27 = (s32[]{:T(128)}, f32[1,128,128]{2,1,0:T(8,128)S(1)}, f32[1,128]{1,0:T(1,128)S(1)}, s32[]{:T(128)}, bf16[64,1,128,128]{3,2,1,0:T(8,128)(2,1)}, /*inde...) while((s32[]{:T(128)}, f32[1,128,128]{2,1,0:T(8,128)S(1)}, ...), condition=%wide.region_21.22_spmd, body=%wide.region_20.21_spmd.sunk | while | flops 33030 | bytes 165283 | solution.py:32
  441.9 0.8 convert_add_fusion.10
  442.7 0.8 convert_add_fusion.10
  443.5 0.8 convert_add_fusion.10
  444.3 0.8 convert_add_fusion.10
  445.1 0.8 convert_add_fusion.10
  446.0 0.8 convert_add_fusion.10
  446.8 0.8 convert_add_fusion.10
  447.6 0.8 convert_add_fusion.10
  448.4 0.8 convert_add_fusion.10
  449.2 0.8 convert_add_fusion.10
  453.3 0.8 convert_add_fusion.10
  454.1 0.8 convert_add_fusion.10
  454.9 0.8 convert_add_fusion.10
  455.8 0.8 convert_add_fusion.10
  456.6 0.8 convert_add_fusion.10
  457.4 0.8 convert_add_fusion.10
  458.2 0.8 convert_add_fusion.10
  459.0 0.8 convert_add_fusion.10
  459.8 0.8 convert_add_fusion.10
  461.5 0.8 convert_add_fusion.10
  462.3 0.8 convert_add_fusion.10
  463.1 0.8 convert_add_fusion.10
  464.8 0.8 convert_add_fusion.10
  465.6 0.8 convert_add_fusion.10
  467.2 0.8 convert_add_fusion.10
  468.0 0.8 convert_add_fusion.10
  468.8 0.8 convert_add_fusion.10
  469.7 0.8 convert_add_fusion.10
  470.5 0.8 convert_add_fusion.10
  472.1 0.8 convert_add_fusion.10
  472.9 0.8 convert_add_fusion.10
  473.7 0.8 convert_add_fusion.10
  474.6 0.8 convert_add_fusion.10
  475.4 0.8 convert_add_fusion.10
  478.6 0.8 convert_add_fusion.10
  479.5 0.8 convert_add_fusion.10
  480.3 0.8 convert_add_fusion.10
  481.1 0.8 convert_add_fusion.10
  486.0 0.8 convert_add_fusion.10
  491.7 0.8 convert_add_fusion.10
  492.5 0.8 convert_add_fusion.10
  493.8 274.0 %psum.22 = f32[128,64]{0,1:T(8,128)} all-reduce(f32[128,64]{0,1:T(8,128)S(1)} %convolution_bitcast_fusion.3), channel_id=1, replica_groups=mesh['seq'=64,'head'=8] {'seq'}, use_global_device_ids=true, to_apply=%region_24.25 | all-reduce | flops 8192 | bytes 65536 | tf_op jit(solution)/shard_map/psum | solution.py:199
  767.7 1.7 copy.144
  (155 shorter events, 25.6 us)
Async XLA Ops:
  7.2 0.7 copy-start
  7.2 120.4 %copy-start.1 = (bf16[144,128]{1,0:T(8,128)(2,1)S(1)}, bf16[144,128]{1,0:T(8,128)(2,1)}, u32[]{:S(2)}) copy-start(bf16[144,128]{1,0:T(8,128)(2,1)} %param.13) | copy-start | bytes 110596
  7.2 140.4 %all-gather.12.cloned.1.call-start = ((), (), s32[]{:S(2)}) async-start(), calls=%async_computation.3 | async-start | bytes 2129920 | tf_op jit(solution)/shard_map/all_gather | solution.py:17
  8.8 23.1 %copy-start.5 = (f32[144]{0:T(256)}, f32[144]{0:T(256)S(1)}, u32[]{:S(2)}) copy-start(f32[144]{0:T(256)S(1)} %get-tuple-element.190) | copy-start | bytes 1732
  8.9 23.0 %copy-start.7 = (f32[144]{0:T(256)}, f32[144]{0:T(256)S(1)}, u32[]{:S(2)}) copy-start(f32[144]{0:T(256)S(1)} %get-tuple-element.187) | copy-start | bytes 1732
  8.9 23.0 %copy-start.9 = (f32[144]{0:T(256)}, f32[144]{0:T(256)S(1)}, u32[]{:S(2)}) copy-start(f32[144]{0:T(256)S(1)} %get-tuple-element.188) | copy-start | bytes 1732
  10.5 221.0 %all-gather.10.cloned.1.call-start = ((), (), s32[]{:S(2)}) async-start(), calls=%async_computation.1 | async-start | bytes 2396160 | tf_op jit(solution)/shard_map/all_gather | solution.py:96
  13.8 217.8 %all-to-all-start = ((bf16[64,144,128]{2,1,0:T(8,128)(2,1)}), bf16[64,144,128]{2,1,0:T(8,128)(2,1)}, u32[]{:S(2)}, u32[]{:S(2)}) async-start(bf16[64,144,128]{2,1,0:T(8,128)(2,1)} %stack.2), calls=%async_computation | async-start | bytes 4718592 | tf_op jit(solution)/shard_map/all_to_all | solution.py:99
  30.6 411.2 %all-gather.14.cloned.1.call-start = ((), (), s32[]{:S(2)}) async-start(), calls=%async_computation.4 | async-start | bytes 2129920 | tf_op jit(solution)/shard_map/all_gather | solution.py:17
  30.6 1.3 copy-start.11
  127.2 104.3 %copy-start.2 = (bf16[8,144,64]{1,2,0:T(8,128)(2,1)}, bf16[8,144,64]{1,2,0:T(8,128)(2,1)S(1)}, u32[]{:S(2)}) copy-start(bf16[8,144,64]{1,2,0:T(8,128)(2,1)S(1)} %get-tuple-element.233) | copy-start | bytes 442372
  294.0 102.6 %copy-start.12 = (bf16[144,1024]{1,0:T(8,128)(2,1)S(1)}, bf16[144,1024]{1,0:T(8,128)(2,1)}, u32[]{:S(2)}) copy-start(bf16[144,1024]{1,0:T(8,128)(2,1)} %param.11) | copy-start | bytes 884740
  294.0 103.7 %copy-start.3 = (bf16[8,144,64]{1,2,0:T(8,128)(2,1)S(1)}, bf16[8,144,64]{1,2,0:T(8,128)(2,1)}, u32[]{:S(2)}) copy-start(bf16[8,144,64]{1,2,0:T(8,128)(2,1)} %copy-done.2) | copy-start | bytes 442372
  296.8 196.7 %copy-start.6 = (f32[144]{0:T(256)S(1)}, f32[144]{0:T(256)}, u32[]{:S(2)}) copy-start(f32[144]{0:T(256)} %copy-done.5) | copy-start | bytes 1732
  296.8 196.7 %copy-start.8 = (f32[144]{0:T(256)S(1)}, f32[144]{0:T(256)}, u32[]{:S(2)}) copy-start(f32[144]{0:T(256)} %copy-done.7) | copy-start | bytes 1732
  296.8 196.7 %copy-start.10 = (f32[144]{0:T(256)S(1)}, f32[144]{0:T(256)}, u32[]{:S(2)}) copy-start(f32[144]{0:T(256)} %copy-done.9) | copy-start | bytes 1732
  297.0 196.6 %copy-start.4 = (bf16[144,128]{1,0:T(8,128)(2,1)S(1)}, bf16[144,128]{1,0:T(8,128)(2,1)}, u32[]{:S(2)}) copy-start(bf16[144,128]{1,0:T(8,128)(2,1)} %param.12) | copy-start | bytes 110596
  299.0 468.8 %all-reduce.2.cloned.1.call-start = ((), (), s32[]{:S(2)}) async-start(), calls=%async_computation.2 | async-start | bytes 524288 | tf_op jit(solution)/shard_map/psum | solution.py:199
Sparse Core Ops, SparseCore 0:
  11.6 135.8 all-gather.11
  150.6 80.8 all-gather.9
  299.1 80.1 all-gather.13
  441.3 147.4 all-reduce.1
